TPU v7x, 32 devices: a whole 2x2x4 slice. The times are simulated.
32 devices in a mesh: dp: 8 (over y, x, core), seq: 4 (over z).
Axes of the slice: x: 2, y: 2, z: 4, core: 2. Of those that a mesh axis runs over, the one named last changes fastest.
Arguments:
- latents_in: bfloat16 [16, 256, 768], P('dp', 'seq'), may hold values from -6 to 6
- conditioning: bfloat16 [16, 768], P('dp'), may hold values from -4 to 4
- out_cotangent: bfloat16 [16, 256, 768], P('dp', 'seq'), may hold values from -6 to 6
- modulation_weight: bfloat16 [768, 4608], P(('dp', 'seq')), may hold values from -0.21875 to 0.21875
- modulation_bias: bfloat16 [4608], P(('dp', 'seq')), may hold values from -3 to 3
- qkv_weight: bfloat16 [768, 2304], P(('dp', 'seq')), may hold values from -0.21875 to 0.21875
- qv_bias: bfloat16 [1536], P(('dp', 'seq')), may hold values from -3 to 3
- proj_weight: bfloat16 [768, 768], P(('dp', 'seq')), may hold values from -0.875 to 0.875
- proj_bias: bfloat16 [768], P(('dp', 'seq')), may hold values from -2 to 2
- mlp_in_weight: bfloat16 [768, 3072], P(('dp', 'seq')), may hold values from -0.21875 to 0.21875
- mlp_in_bias: bfloat16 [3072], P(('dp', 'seq')), may hold values from -3 to 3
- mlp_out_weight: bfloat16 [3072, 768], P(('dp', 'seq')), may hold values from -0.109375 to 0.109375
- mlp_out_bias: bfloat16 [768], P(('dp', 'seq')), may hold values from -3 to 3
Outputs:
- block_out: float32 [16, 256, 768], P('dp', 'seq')
- grad_latents: float32 [16, 256, 768], P('dp', 'seq')
- grad_conditioning: float32 [16, 768], P('dp')
- grad_modulation_weight: float32 [768, 4608], P(('dp', 'seq'))
- grad_modulation_bias: float32 [4608], P(('dp', 'seq'))
- grad_qkv_weight: float32 [768, 2304], P(('dp', 'seq'))
- grad_qv_bias: float32 [1536], P(('dp', 'seq'))
- grad_proj_weight: float32 [768, 768], P(('dp', 'seq'))
- grad_proj_bias: float32 [768], P(('dp', 'seq'))
- grad_mlp_in_weight: float32 [768, 3072], P(('dp', 'seq'))
- grad_mlp_in_bias: float32 [3072], P(('dp', 'seq'))
- grad_mlp_out_weight: float32 [3072, 768], P(('dp', 'seq'))
- grad_mlp_out_bias: float32 [768], P(('dp', 'seq'))
All inputs are finite; a program needn't handle non-finite values.
Results may differ from a plain program's by a relative error of at most 0.012.
The roundings to bfloat16 on the way count: a program that leaves them out, or rounds other values in their place, can miss the bound.
Values may be sent and summed in bfloat16 or wider, within the bound.
A program may use at most 192 MiB of HBM per device.

v0:
```python
import math

import jax
import jax.numpy as jnp
from jax import lax
from jax.sharding import PartitionSpec as P

HEADS = 12


EPS = 1e-06
GELU_C = math.sqrt(2.0 / math.pi)


def layer_norm(inputs):
    center = inputs - jnp.mean(inputs, axis=-1, keepdims=True)
    inverse = lax.rsqrt(jnp.mean(center * center, axis=-1, keepdims=True) + EPS)
    return (center * inverse, inverse)


def norm_back(upstream, normed, inverse):
    return inverse * (
        upstream
        - jnp.mean(upstream, axis=-1, keepdims=True)
        - normed * jnp.mean(upstream * normed, axis=-1, keepdims=True)
    )


def gelu_pair(inputs):
    tangent = jnp.tanh(GELU_C * (inputs + 0.044715 * inputs * inputs * inputs))
    value = 0.5 * inputs * (1.0 + tangent)
    slope = 0.5 * (1.0 + tangent) + 0.5 * inputs * (1.0 - tangent * tangent) * GELU_C * (
        1.0 + 3.0 * 0.044715 * inputs * inputs
    )
    return (value, slope)


def matmul(left, right):
    return jnp.dot(left, right, preferred_element_type=jnp.float32)


def matmul_right_t(left, right):
    return lax.dot_general(
        left, right, (((1,), (1,)), ((), ())), preferred_element_type=jnp.float32
    )


def matmul_left_t(left, right):
    return lax.dot_general(
        left, right, (((0,), (0,)), ((), ())), preferred_element_type=jnp.float32
    )


def exact_right_t(left, right):
    return lax.dot_general(
        left,
        right,
        (((1,), (1,)), ((), ())),
        precision=lax.Precision.HIGHEST,
        preferred_element_type=jnp.float32,
    )


def exact_left_t(left, right):
    return lax.dot_general(
        left,
        right,
        (((0,), (0,)), ((), ())),
        precision=lax.Precision.HIGHEST,
        preferred_element_type=jnp.float32,
    )


def local(
    latents_in,
    conditioning,
    out_cotangent,
    modulation_weight,
    modulation_bias,
    qkv_weight,
    qv_bias,
    proj_weight,
    proj_bias,
    mlp_in_weight,
    mlp_in_bias,
    mlp_out_weight,
    mlp_out_bias,
):
    lat_count, local_len, width = latents_in.shape
    head_size = width // HEADS
    factor = head_size ** (-0.5)
    tokens = lat_count * local_len
    cond_float = conditioning.astype(jnp.float32)
    cond_act = jax.nn.silu(cond_float).astype(jnp.bfloat16)
    gathered = (
        lax.all_gather(qkv_weight, ("dp", "seq"), axis=0, tiled=True),
        lax.all_gather(proj_weight, ("dp", "seq"), axis=0, tiled=True),
        lax.all_gather(mlp_in_weight, ("dp", "seq"), axis=0, tiled=True),
        lax.all_gather(mlp_out_weight, ("dp", "seq"), axis=0, tiled=True),
        lax.all_gather(modulation_weight, ("dp", "seq"), axis=0, tiled=True),
        lax.all_gather(qv_bias, ("dp", "seq"), axis=0, tiled=True),
        lax.all_gather(proj_bias, ("dp", "seq"), axis=0, tiled=True),
        lax.all_gather(mlp_in_bias, ("dp", "seq"), axis=0, tiled=True),
        lax.all_gather(mlp_out_bias, ("dp", "seq"), axis=0, tiled=True),
        lax.all_gather(modulation_bias, ("dp", "seq"), axis=0, tiled=True),
    )
    qkv_full, proj_full, in_full, out_full = (gathered[0], gathered[1], gathered[2], gathered[3])
    qv_full, proj_bias_full, in_bias_full, out_bias_full = (
        gathered[5],
        gathered[6],
        gathered[7],
        gathered[8],
    )
    modulation = matmul(cond_act, gathered[4]) + gathered[9].astype(jnp.float32)
    shift_attn, scale_attn, gate_attn, shift_mlp, scale_mlp, gate_mlp = [
        piece[:, None, :] for piece in jnp.split(modulation, 6, axis=1)
    ]
    resid = latents_in.astype(jnp.float32)
    normed_attn, inverse_attn = layer_norm(resid)
    act_attn = (
        (normed_attn * (1.0 + scale_attn) + shift_attn).astype(jnp.bfloat16).reshape(tokens, width)
    )
    projected = matmul(act_attn, qkv_full)
    qv_float = qv_full.astype(jnp.float32)
    queries = (
        (projected[:, :width] + qv_float[:width])
        .astype(jnp.bfloat16)
        .reshape(lat_count, local_len, HEADS, head_size)
    )
    keys_local = (
        projected[:, width : 2 * width].astype(jnp.bfloat16).reshape(lat_count, local_len, width)
    )
    values_local = (
        (projected[:, 2 * width :] + qv_float[width:])
        .astype(jnp.bfloat16)
        .reshape(lat_count, local_len, width)
    )
    keys_all, values_all = (
        lax.all_gather(keys_local, "seq", axis=1, tiled=True),
        lax.all_gather(values_local, "seq", axis=1, tiled=True),
    )
    keys_all = keys_all.reshape(lat_count, -1, HEADS, head_size)
    values_all = values_all.reshape(lat_count, -1, HEADS, head_size)
    scores = (
        jnp.einsum("bqhd,bkhd->bhqk", queries, keys_all, preferred_element_type=jnp.float32)
        * factor
    )
    top = jnp.max(scores, axis=-1, keepdims=True)
    log_total = top + jnp.log(jnp.sum(jnp.exp(scores - top), axis=-1, keepdims=True))
    probs = jnp.exp(scores - log_total).astype(jnp.bfloat16)
    attended = (
        jnp.einsum("bhqk,bkhd->bqhd", probs, values_all, preferred_element_type=jnp.float32)
        .astype(jnp.bfloat16)
        .reshape(tokens, width)
    )
    attn_branch = (matmul(attended, proj_full) + proj_bias_full.astype(jnp.float32)).reshape(
        lat_count, local_len, width
    )
    mid = resid + gate_attn * attn_branch
    normed_mlp, inverse_mlp = layer_norm(mid)
    act_mlp = (
        (normed_mlp * (1.0 + scale_mlp) + shift_mlp).astype(jnp.bfloat16).reshape(tokens, width)
    )
    pre_gelu = matmul(act_mlp, in_full) + in_bias_full.astype(jnp.float32)
    gelu_value, gelu_slope = gelu_pair(pre_gelu)
    gelu_out = gelu_value.astype(jnp.bfloat16)
    mlp_branch = (matmul(gelu_out, out_full) + out_bias_full.astype(jnp.float32)).reshape(
        lat_count, local_len, width
    )
    block_out = mid + gate_mlp * mlp_branch
    back_qkv, back_proj, back_in, back_out, back_mod = (
        lax.all_gather(qkv_weight, ("dp", "seq"), axis=0, tiled=True),
        lax.all_gather(proj_weight, ("dp", "seq"), axis=0, tiled=True),
        lax.all_gather(mlp_in_weight, ("dp", "seq"), axis=0, tiled=True),
        lax.all_gather(mlp_out_weight, ("dp", "seq"), axis=0, tiled=True),
        lax.all_gather(modulation_weight, ("dp", "seq"), axis=0, tiled=True),
    )
    cot = out_cotangent.astype(jnp.float32)
    grad_gate_mlp = jnp.sum(cot * mlp_branch, axis=1)
    grad_mlp = (cot * gate_mlp).reshape(tokens, width)
    grad_mlp_b = grad_mlp.astype(jnp.bfloat16)
    grad_out_weight = matmul_left_t(gelu_out, grad_mlp_b)
    grad_out_bias = jnp.sum(grad_mlp, axis=0)
    grad_pre = matmul_right_t(grad_mlp_b, back_out) * gelu_slope
    grad_pre_b = grad_pre.astype(jnp.bfloat16)
    grad_in_weight = matmul_left_t(act_mlp, grad_pre_b)
    grad_in_bias = jnp.sum(grad_pre, axis=0)
    grad_act_mlp = matmul_right_t(grad_pre_b, back_in).reshape(lat_count, local_len, width)
    grad_shift_mlp = jnp.sum(grad_act_mlp, axis=1)
    grad_scale_mlp = jnp.sum(grad_act_mlp * normed_mlp, axis=1)
    grad_mid = cot + norm_back(grad_act_mlp * (1.0 + scale_mlp), normed_mlp, inverse_mlp)
    grad_gate_attn = jnp.sum(grad_mid * attn_branch, axis=1)
    grad_attn = (grad_mid * gate_attn).reshape(tokens, width)
    grad_attn_b = grad_attn.astype(jnp.bfloat16)
    grad_proj_weight = matmul_left_t(attended, grad_attn_b)
    grad_proj_bias = jnp.sum(grad_attn, axis=0)
    grad_attended = (
        matmul_right_t(grad_attn_b, back_proj)
        .astype(jnp.bfloat16)
        .reshape(lat_count, local_len, HEADS, head_size)
    )
    recomputed = (
        jnp.einsum("bqhd,bkhd->bhqk", queries, keys_all, preferred_element_type=jnp.float32)
        * factor
    )
    weights_exact = jnp.exp(recomputed - log_total)
    grad_probs = jnp.einsum(
        "bqhd,bkhd->bhqk", grad_attended, values_all, preferred_element_type=jnp.float32
    )
    inner = jnp.sum(weights_exact * grad_probs, axis=-1, keepdims=True)
    grad_scores = (weights_exact * (grad_probs - inner) * factor).astype(jnp.bfloat16)
    grad_queries = jnp.einsum(
        "bhqk,bkhd->bqhd", grad_scores, keys_all, preferred_element_type=jnp.float32
    ).reshape(tokens, width)
    weights_b = weights_exact.astype(jnp.bfloat16)
    grad_values_all = jnp.einsum(
        "bhqk,bqhd->bkhd", weights_b, grad_attended, preferred_element_type=jnp.float32
    )
    grad_keys_all = jnp.einsum(
        "bhqk,bqhd->bkhd", grad_scores, queries, preferred_element_type=jnp.float32
    )
    grad_keys, grad_values = (
        lax.psum_scatter(
            grad_keys_all.reshape(lat_count, -1, width), "seq", scatter_dimension=1, tiled=True
        ),
        lax.psum_scatter(
            grad_values_all.reshape(lat_count, -1, width), "seq", scatter_dimension=1, tiled=True
        ),
    )
    grad_keys = grad_keys.reshape(tokens, width)
    grad_values = grad_values.reshape(tokens, width)
    grad_qkv_b = jnp.concatenate([grad_queries, grad_keys, grad_values], axis=1).astype(
        jnp.bfloat16
    )
    grad_qkv_weight = matmul_left_t(act_attn, grad_qkv_b)
    grad_qv_bias = jnp.concatenate([jnp.sum(grad_queries, axis=0), jnp.sum(grad_values, axis=0)])
    grad_act_attn = matmul_right_t(grad_qkv_b, back_qkv).reshape(lat_count, local_len, width)
    grad_shift_attn = jnp.sum(grad_act_attn, axis=1)
    grad_scale_attn = jnp.sum(grad_act_attn * normed_attn, axis=1)
    grad_latents = grad_mid + norm_back(
        grad_act_attn * (1.0 + scale_attn), normed_attn, inverse_attn
    )
    grad_mod_part = jnp.concatenate(
        [
            grad_shift_attn,
            grad_scale_attn,
            grad_gate_attn,
            grad_shift_mlp,
            grad_scale_mlp,
            grad_gate_mlp,
        ],
        axis=1,
    )
    grad_modulation = lax.psum(grad_mod_part, "seq")
    sigma = jax.nn.sigmoid(cond_float)
    silu_slope = sigma * (1.0 + cond_float * (1.0 - sigma))
    mod_blocks = jnp.split(grad_modulation, 6, axis=1)
    weight_blocks = jnp.split(back_mod, 6, axis=1)
    through = jnp.zeros((lat_count, width), jnp.float32)
    for grad_block, weight_block in zip(mod_blocks, weight_blocks):
        through = through + exact_right_t(grad_block, weight_block.astype(jnp.float32))
    grad_conditioning = through * silu_slope
    local_mod_weight = exact_left_t(cond_act.astype(jnp.float32), grad_mod_part)
    local_mod_bias = jnp.sum(grad_mod_part, axis=0)
    summed = (
        lax.psum_scatter(grad_qkv_weight, ("dp", "seq"), scatter_dimension=0, tiled=True),
        lax.psum_scatter(grad_proj_weight, ("dp", "seq"), scatter_dimension=0, tiled=True),
        lax.psum_scatter(grad_in_weight, ("dp", "seq"), scatter_dimension=0, tiled=True),
        lax.psum_scatter(grad_out_weight, ("dp", "seq"), scatter_dimension=0, tiled=True),
        lax.psum_scatter(local_mod_weight, ("dp", "seq"), scatter_dimension=0, tiled=True),
        lax.psum_scatter(grad_qv_bias, ("dp", "seq"), scatter_dimension=0, tiled=True),
        lax.psum_scatter(grad_proj_bias, ("dp", "seq"), scatter_dimension=0, tiled=True),
        lax.psum_scatter(grad_in_bias, ("dp", "seq"), scatter_dimension=0, tiled=True),
        lax.psum_scatter(grad_out_bias, ("dp", "seq"), scatter_dimension=0, tiled=True),
        lax.psum_scatter(local_mod_bias, ("dp", "seq"), scatter_dimension=0, tiled=True),
    )
    owned_qkv, owned_proj, owned_in, owned_out, grad_modulation_weight = (
        summed[0],
        summed[1],
        summed[2],
        summed[3],
        summed[4],
    )
    owned_qv, owned_proj_bias, owned_in_bias, owned_out_bias, grad_modulation_bias = (
        summed[5],
        summed[6],
        summed[7],
        summed[8],
        summed[9],
    )
    return (
        block_out,
        grad_latents,
        grad_conditioning,
        grad_modulation_weight,
        grad_modulation_bias,
        owned_qkv,
        owned_qv,
        owned_proj,
        owned_proj_bias,
        owned_in,
        owned_in_bias,
        owned_out,
        owned_out_bias,
    )


def solution(mesh):
    placed = (
        P("dp", "seq", None),
        P("dp", None),
        P("dp", "seq", None),
        P(("dp", "seq"), None),
        P(("dp", "seq")),
        P(("dp", "seq"), None),
        P(("dp", "seq")),
        P(("dp", "seq"), None),
        P(("dp", "seq")),
        P(("dp", "seq"), None),
        P(("dp", "seq")),
        P(("dp", "seq"), None),
        P(("dp", "seq")),
    )
    return jax.shard_map(
        local,
        mesh=mesh,
        in_specs=placed,
        out_specs=(
            P("dp", "seq", None),
            P("dp", "seq", None),
            P("dp", None),
            P(("dp", "seq"), None),
            P(("dp", "seq")),
            P(("dp", "seq"), None),
            P(("dp", "seq")),
            P(("dp", "seq"), None),
            P(("dp", "seq")),
            P(("dp", "seq"), None),
            P(("dp", "seq")),
            P(("dp", "seq"), None),
            P(("dp", "seq")),
        ),
        check_vma=False,
    )
```

profile of v0, /device:TPU:0, one launch (start us, length us, event | category | flops | bytes accessed | tf_op | source)
XLA Modules:
  0.0 1130.0 jit_solution(17478672011295410274)
XLA Ops:
  14.9 42.7 %all-reduce.11 = (bf16[4608]{0:T(1024)(128)(2,1)S(1)}, bf16[1536]{0:T(1024)(128)(2,1)S(1)}, bf16[768]{0:T(1024)(128)(2,1)S(1)}, bf16[768]{0:T(1024)(128)(2,1)S(1)}, bf16[3072]{0:T(1024)(128)(2,1)S(1)}) all-reduce(bf16[4608]{0:T(1024)(128)(2,1)S(1)} %dynamic-update-slice, ...), channel_id=1, replica_groups=mesh['dp'=8,'seq'=4] {'dp','seq'}, use_global_device_ids=true, to_apply=%add | all-reduce | flops 10752 | bytes 43008
  61.1 24.5 %all-gather.6.cloned.1.call-done = bf16[768,4608]{1,0:T(8,128)(2,1)} async-done(((bf16[24,4608]{1,0:T(8,128)(2,1)}), bf16[768,4608]{1,0:T(8,128)(2,1)}) %all-gather.6.cloned.1.call-update) | async-done | bytes 7077904 | tf_op jit(solution)/shard_map/all_gather | solution.py:100
  85.6 4.0 convolution_add_fusion
  90.4 56.5 %all-gather.8.cloned.1.call-done = bf16[768,2304]{1,0:T(8,128)(2,1)} async-done(((bf16[24,2304]{1,0:T(8,128)(2,1)}), bf16[768,2304]{1,0:T(8,128)(2,1)}) %all-gather.8.cloned.1.call-update) | async-done | bytes 3538960 | tf_op jit(solution)/shard_map/all_gather | solution.py:96
  147.0 2.6 fusion.120
  151.2 18.9 %all_gather.46 = bf16[2,256,768]{2,1,0:T(8,128)(2,1)S(1)} all-gather(bf16[2,64,768]{2,1,0:T(8,128)(2,1)S(1)} %bitcast.98), channel_id=1, replica_groups=mesh['dp'=8,'seq'=4] {'seq'}, dimensions={1}, use_global_device_ids=true | all-gather | bytes 983040 | tf_op jit(solution)/shard_map/all_gather | solution.py:139
  170.3 19.6 %all_gather.45 = bf16[2,256,768]{2,1,0:T(8,128)(2,1)S(1)} all-gather(bf16[2,64,768]{2,1,0:T(8,128)(2,1)S(1)} %bitcast.97), channel_id=1, replica_groups=mesh['dp'=8,'seq'=4] {'seq'}, dimensions={1}, use_global_device_ids=true | all-gather | bytes 983040 | tf_op jit(solution)/shard_map/all_gather | solution.py:140
  190.2 1.8 fusion.116
  193.7 9.8 all-gather.10.cloned.1.call-done
  203.5 1.6 convolution_add_fusion.2
  206.5 62.3 %all-gather.12.cloned.1.call-done = bf16[768,3072]{1,0:T(8,128)(2,1)} async-done(((bf16[24,3072]{1,0:T(8,128)(2,1)}), bf16[768,3072]{1,0:T(8,128)(2,1)}) %all-gather.12.cloned.1.call-update) | async-done | bytes 4718608 | tf_op jit(solution)/shard_map/all_gather | solution.py:98
  268.7 3.1 convolution_add_fusion.1
  271.9 61.4 %all-gather.14.cloned.1.call-done = bf16[3072,768]{1,0:T(8,128)(2,1)} async-done(((bf16[96,768]{1,0:T(8,128)(2,1)}), bf16[3072,768]{1,0:T(8,128)(2,1)}) %all-gather.14.cloned.1.call-update) | async-done | bytes 4718608 | tf_op jit(solution)/shard_map/all_gather | solution.py:99
  333.3 5.0 fusion.119
  338.3 2.4 fusion.76
  341.3 1.3 div.39
  342.6 2.0 fusion.77
  344.6 3.5 convolution_add_fusion.3
  348.2 1.6 multiply_reduce_fusion.4
  353.0 1.4 copy.70
  354.4 2.7 fusion.121
  357.1 11.6 %fusion.10 = f32[2,12,64,256]{3,2,1,0:T(8,128)} fusion(bf16[2,64,12,64]{1,3,2,0:T(8,128)(2,1)} %copy.68, f32[2,12,64,256]{3,2,1,0:T(8,128)} %fusion.121, f32[2,12,64,256]{3,2,1,0:T(8,128)S(1)} %get-tuple-element.54, f32[2,12,64]{2,1,0:T(8,128)} %copy-done.30), kind=kOutput, calls=%fused_computation.17 | convolution fusion | flops 53085952 | bytes 4921344 | tf_op jit(solution)/shard_map/bhqk,bqhd->bkhd/dot_general | solution.py:219
  368.7 3.0 copy.69
  372.0 2.3 fusion.84
  374.3 3.0 copy.71
  378.4 1.8 fusion.122
  380.3 11.2 fusion.112
  392.0 13.6 %reduce-scatter.8.cloned.1.call-done = f32[2,64,768]{2,1,0:T(8,128)} async-done(((f32[2,256,768]{2,1,0:T(8,128)}), f32[2,64,768]{2,1,0:T(8,128)}) %reduce-scatter.8.cloned.1.call-update) | async-done | bytes 393232 | tf_op jit(solution)/shard_map/reduce_scatter | solution.py:223
  406.8 35.4 %reduce-scatter.10.cloned.1.call-done = f32[2,64,768]{2,1,0:T(8,128)} async-done(((f32[2,256,768]{2,1,0:T(8,128)}), f32[2,64,768]{2,1,0:T(8,128)}) %reduce-scatter.10.cloned.1.call-update) | async-done | bytes 393232 | tf_op jit(solution)/shard_map/reduce_scatter | solution.py:226
  442.3 1.8 fusion.113
  444.2 4.0 fusion.82
  449.2 5.1 fusion.110
  455.5 5.0 fusion.78
  460.8 1.7 copy-done.1
  462.6 3.1 fusion.75
  466.5 8.9 fusion.105
  476.3 40.0 %all-reduce.10 = (f32[4608]{0:T(1024)S(1)}, f32[1536]{0:T(1024)S(1)}, f32[768]{0:T(1024)S(1)}, f32[3072]{0:T(1024)S(1)}, f32[768]{0:T(1024)S(1)}) all-reduce(f32[4608]{0:T(1024)S(1)} %reduce_sum.216, f32[1536]{0:T(1024)S(1)} %pad_maximum_fusion.3, f32[768]{0:T(1024)S(1)} %copy-done.45, ...), channel_id=5, replica_groups=mesh['dp'=8,'seq'=4] {'dp','seq'}, use_global_device_ids=true, to_apply=%region_22.23.clone | all-reduce | flops 10752 | bytes 86016
  519.3 18.4 %psum.7 = f32[2,4608]{1,0:T(2,128)S(1)} all-reduce(f32[2,4608]{1,0:T(2,128)S(1)} %constant_dynamic-update-slice_fusion), channel_id=1, replica_groups=mesh['dp'=8,'seq'=4] {'seq'}, use_global_device_ids=true, to_apply=%region_19.20 | all-reduce | flops 9216 | bytes 73728 | tf_op jit(solution)/shard_map/psum | solution.py:254
  537.8 2.3 fusion.19
  540.1 2.3 fusion.21
  542.4 2.3 fusion.23
  544.8 2.4 fusion.25
  547.2 2.3 fusion.27
  549.5 3.0 fusion.46
  553.4 118.2 %reduce-scatter.14.cloned.1.call-done = f32[24,2304]{1,0:T(8,128)} async-done(((f32[768,2304]{1,0:T(8,128)}), f32[24,2304]{1,0:T(8,128)}) %reduce-scatter.14.cloned.1.call-update) | async-done | bytes 221200 | tf_op jit(solution)/shard_map/reduce_scatter | solution.py:266
  671.6 141.5 %reduce-scatter.20.cloned.1.call-done = f32[96,768]{1,0:T(8,128)} async-done(((f32[3072,768]{1,0:T(8,128)}), f32[96,768]{1,0:T(8,128)}) %reduce-scatter.20.cloned.1.call-update) | async-done | bytes 294928 | tf_op jit(solution)/shard_map/reduce_scatter | solution.py:269
  813.1 141.7 %reduce-scatter.18.cloned.1.call-done = f32[24,3072]{1,0:T(8,128)} async-done(((f32[768,3072]{1,0:T(8,128)}), f32[24,3072]{1,0:T(8,128)}) %reduce-scatter.18.cloned.1.call-update) | async-done | bytes 294928 | tf_op jit(solution)/shard_map/reduce_scatter | solution.py:268
  954.8 168.4 %reduce-scatter.12.cloned.1.call-done = f32[24,4608]{1,0:T(8,128)} async-done(((f32[768,4608]{1,0:T(8,128)}), f32[24,4608]{1,0:T(8,128)}) %reduce-scatter.12.cloned.1.call-update) | async-done | bytes 442384 | tf_op jit(solution)/shard_map/reduce_scatter | solution.py:270
  (204 shorter events, 31.8 us)
Async XLA Ops:
  7.2 78.4 %all-gather.6.cloned.1.call-start = ((), (), s32[]{:S(2)}) async-start(), calls=%async_computation.7 | async-start | bytes 7299072 | tf_op jit(solution)/shard_map/all_gather | solution.py:100
  7.9 139.1 %all-gather.8.cloned.1.call-start = ((), (), s32[]{:S(2)}) async-start(), calls=%async_computation.8 | async-start | bytes 3649536 | tf_op jit(solution)/shard_map/all_gather | solution.py:96
  8.7 194.8 %all-gather.10.cloned.1.call-start = ((), (), s32[]{:S(2)}) async-start(), calls=%async_computation.9 | async-start | bytes 1216512 | tf_op jit(solution)/shard_map/all_gather | solution.py:97
  9.4 259.3 %all-gather.12.cloned.1.call-start = ((), (), s32[]{:S(2)}) async-start(), calls=%async_computation.10 | async-start | bytes 4866048 | tf_op jit(solution)/shard_map/all_gather | solution.py:98
  10.0 323.3 %all-gather.14.cloned.1.call-start = ((), (), s32[]{:S(2)}) async-start(), calls=%async_computation.11 | async-start | bytes 4866048 | tf_op jit(solution)/shard_map/all_gather | solution.py:99
  10.6 395.1 %reduce-scatter.8.cloned.1.call-start = ((), (), s32[]{:S(2)}) async-start(), calls=%async_computation.12 | async-start | bytes 1966080 | tf_op jit(solution)/shard_map/reduce_scatter | solution.py:223
  59.9 30.3 %copy-start.35 = (f32[2,64]{1,0:T(2,128)}, f32[2,64]{1,0:T(2,128)S(1)}, u32[]{:S(2)}) copy-start(f32[2,64]{1,0:T(2,128)S(1)} %broadcast_multiply_fusion.3) | copy-start | bytes 1540
  61.1 29.2 %copy-start.48 = (f32[2,64]{1,0:T(2,128)}, f32[2,64]{1,0:T(2,128)S(1)}, u32[]{:S(2)}) copy-start(f32[2,64]{1,0:T(2,128)S(1)} %add_rsqrt_fusion.1) | copy-start | bytes 1540
  61.1 29.2 %copy-start.3 = (bf16[2,64,768]{2,1,0:T(8,128)(2,1)S(1)}, bf16[2,64,768]{2,1,0:T(8,128)(2,1)}, u32[]{:S(2)}) copy-start(bf16[2,64,768]{2,1,0:T(8,128)(2,1)} %param.13) | copy-start | bytes 589828
  90.4 59.2 %copy-start.17 = (bf16[2,64,768]{2,1,0:T(8,128)(2,1)}, bf16[2,64,768]{2,1,0:T(8,128)(2,1)S(1)}, u32[]{:S(2)}) copy-start(bf16[2,64,768]{2,1,0:T(8,128)(2,1)S(1)} %fusion.65) | copy-start | bytes 589828
  170.3 21.7 %copy-start.16 = (bf16[2,256,768]{1,2,0:T(8,128)(2,1)}, bf16[2,256,768]{1,2,0:T(8,128)(2,1)S(1)}, u32[]{:S(2)}) copy-start(bf16[2,256,768]{1,2,0:T(8,128)(2,1)S(1)} %copy.62) | copy-start | bytes 2359300
  193.0 12.1 %copy-start.31 = (f32[2,768]{1,0:T(2,128)S(1)}, f32[2,768]{1,0:T(2,128)}, u32[]{:S(2)}) copy-start(f32[2,768]{1,0:T(2,128)} %get-tuple-element.50) | copy-start | bytes 18436
  193.7 11.8 %copy-start.23 = (bf16[128,768]{0,1:T(8,128)(2,1)}, bf16[128,768]{0,1:T(8,128)(2,1)S(1)}, u32[]{:S(2)}) copy-start(bf16[128,768]{0,1:T(8,128)(2,1)S(1)} %reshape.173) | copy-start | bytes 589828
  193.7 11.8 %copy-start.28 = (bf16[2,64,768]{2,1,0:T(8,128)(2,1)S(1)}, bf16[2,64,768]{2,1,0:T(8,128)(2,1)}, u32[]{:S(2)}) copy-start(bf16[2,64,768]{2,1,0:T(8,128)(2,1)} %param.15) | copy-start | bytes 589828
  193.7 11.8 %copy-start.33 = (f32[2,768]{1,0:T(2,128)S(1)}, f32[2,768]{1,0:T(2,128)}, u32[]{:S(2)}) copy-start(f32[2,768]{1,0:T(2,128)} %get-tuple-element.45) | copy-start | bytes 18436
  193.7 11.8 %copy-start.39 = (f32[2,768]{1,0:T(2,128)S(1)}, f32[2,768]{1,0:T(2,128)}, u32[]{:S(2)}) copy-start(f32[2,768]{1,0:T(2,128)} %get-tuple-element.46) | copy-start | bytes 18436
  205.1 63.6 %copy-start.10 = (f32[128,768]{1,0:T(8,128)}, f32[128,768]{1,0:T(8,128)S(1)}, u32[]{:S(2)}) copy-start(f32[128,768]{1,0:T(8,128)S(1)} %convolution_add_fusion.2) | copy-start | bytes 1179652
  205.3 63.4 %copy-start.37 = (f32[2,64]{1,0:T(2,128)}, f32[2,64]{1,0:T(2,128)S(1)}, u32[]{:S(2)}) copy-start(f32[2,64]{1,0:T(2,128)S(1)} %broadcast_multiply_fusion.2) | copy-start | bytes 1540
  205.5 63.2 %copy-start.51 = (f32[2,64]{1,0:T(2,128)}, f32[2,64]{1,0:T(2,128)S(1)}, u32[]{:S(2)}) copy-start(f32[2,64]{1,0:T(2,128)S(1)} %add_rsqrt_fusion) | copy-start | bytes 1540
  333.3 5.0 copy-start
  344.6 3.5 copy-start.8
  344.6 3.5 copy-start.11
  344.6 3.5 copy-start.29
  344.6 3.6 copy-start.32
  344.6 3.6 copy-start.34
  344.6 3.6 copy-start.38
  344.6 3.6 copy-start.52
  344.6 3.6 copy-start.55
  371.7 70.5 %reduce-scatter.10.cloned.1.call-start = ((), (), s32[]{:S(2)}) async-start(), calls=%async_computation.13 | async-start | bytes 1966080 | tf_op jit(solution)/shard_map/reduce_scatter | solution.py:226
  377.4 176.0 %reduce-scatter.16.cloned.1.call-start = ((), (), s32[]{:S(2)}) async-start(), calls=%async_computation.16 | async-start | bytes 2433024 | tf_op jit(solution)/shard_map/reduce_scatter | solution.py:267
  380.2 291.4 %reduce-scatter.14.cloned.1.call-start = ((), (), s32[]{:S(2)}) async-start(), calls=%async_computation.15 | async-start | bytes 7299072 | tf_op jit(solution)/shard_map/reduce_scatter | solution.py:266
  391.5 52.8 %copy-start.18 = (bf16[2,64,768]{2,1,0:T(8,128)(2,1)S(1)}, bf16[2,64,768]{2,1,0:T(8,128)(2,1)}, u32[]{:S(2)}) copy-start(bf16[2,64,768]{2,1,0:T(8,128)(2,1)} %copy-done.17) | copy-start | bytes 589828
  392.0 56.2 %copy-start.21 = (bf16[128,768]{0,1:T(8,128)(2,1)}, bf16[128,768]{0,1:T(8,128)(2,1)S(1)}, u32[]{:S(2)}) copy-start(bf16[128,768]{0,1:T(8,128)(2,1)S(1)} %reshape.179) | copy-start | bytes 589828
  406.8 41.4 %copy-start.19 = (bf16[128,768]{0,1:T(8,128)(2,1)}, bf16[128,768]{0,1:T(8,128)(2,1)S(1)}, u32[]{:S(2)}) copy-start(bf16[128,768]{0,1:T(8,128)(2,1)S(1)} %copy.72) | copy-start | bytes 589828
  444.2 4.0 copy-start.20
  448.3 364.8 %reduce-scatter.20.cloned.1.call-start = ((), (), s32[]{:S(2)}) async-start(), calls=%async_computation.18 | async-start | bytes 9732096 | tf_op jit(solution)/shard_map/reduce_scatter | solution.py:269
  454.4 500.4 %reduce-scatter.18.cloned.1.call-start = ((), (), s32[]{:S(2)}) async-start(), calls=%async_computation.17 | async-start | bytes 9732096 | tf_op jit(solution)/shard_map/reduce_scatter | solution.py:268
  460.5 5.1 copy-start.36
  460.5 6.0 copy-start.44
  460.5 662.6 %reduce-scatter.12.cloned.1.call-start = ((), (), s32[]{:S(2)}) async-start(), calls=%async_computation.14 | async-start | bytes 14598144 | tf_op jit(solution)/shard_map/reduce_scatter | solution.py:270
  462.5 3.9 copy-start.43
  462.5 3.9 copy-start.41
  462.5 3.9 copy-start.40
  462.6 3.9 copy-start.42
  544.7 7.7 copy-start.5
  544.7 7.7 copy-start.7
  544.7 7.7 copy-start.13
  544.8 7.7 copy-start.50
  (21 other events, 29.8 us)
Sparse Core Ops, SparseCore 0:
  10.8 74.7 all-gather.5
  88.4 58.5 all-gather.7
  149.8 53.6 all-gather.9
  206.2 62.5 all-gather.11
  271.4 61.8 all-gather.13
  371.9 33.7 reduce-scatter.7
  407.9 34.2 reduce-scatter.9
  448.1 98.6 reduce-scatter.15
  553.1 118.5 reduce-scatter.13
  678.0 135.1 reduce-scatter.19
  819.6 135.1 reduce-scatter.17
  961.2 161.8 reduce-scatter.11
where the time goes:
time: 1130 us
  waiting for transfers between devices  836 us (74%)
  blocking collectives  140 us (12%)
  matrix products  95.5 us (8%)
  local copies, waits for them, and re-layouts  28.2 us (2%)
  between operations  15 us (1%)
  other arithmetic  14.3 us (1%)
    reduce_scatter x1, waiting for transfers between devices, local(): lax.psum_scatter(local_mod_weight, ('dp', 'seq'), scatter_dimension=0, ti...  168 us
    reduce_scatter x1, waiting for transfers between devices, local(): lax.psum_scatter(grad_in_weight, ('dp', 'seq'), scatter_dimension=0, tile...  142 us
    reduce_scatter x1, waiting for transfers between devices, local(): lax.psum_scatter(grad_out_weight, ('dp', 'seq'), scatter_dimension=0, til...  141 us
    reduce_scatter x1, waiting for transfers between devices, local(): lax.psum_scatter(grad_qkv_weight, ('dp', 'seq'), scatter_dimension=0, til...  118 us
    unnamed x2, blocking collectives  82.7 us
    all_gather x1, waiting for transfers between devices, local(): lax.all_gather(mlp_in_weight, ('dp', 'seq'), axis=0, tiled=True)  62.3 us
    all_gather x1, waiting for transfers between devices, local(): lax.all_gather(mlp_out_weight, ('dp', 'seq'), axis=0, tiled=True)  61.4 us
    all_gather x1, waiting for transfers between devices, local(): lax.all_gather(qkv_weight, ('dp', 'seq'), axis=0, tiled=True)  56.5 us
  transfers between devices with their start and end apart: 12, of which 11 were waited for; matrix products, arithmetic and copies ran while one was open for 8% of the time, Pallas kernels for 0%

commit v1 on v0

--- a/solution.py
+++ b/solution.py
@@ -69,6 +69,14 @@
         precision=lax.Precision.HIGHEST,
         preferred_element_type=jnp.float32,
     )
+
+
+def reduce_rows(grad):
+    within = lax.psum_scatter(
+        grad.astype(jnp.bfloat16), "dp", scatter_dimension=0, tiled=True
+    )
+    across = lax.psum_scatter(within, "seq", scatter_dimension=0, tiled=True)
+    return across.astype(jnp.float32)
 
 
 def local(
@@ -90,28 +98,32 @@
     head_size = width // HEADS
     factor = head_size ** (-0.5)
     tokens = lat_count * local_len
+    axes = ("dp", "seq")
+    parts = lax.axis_size("dp") * lax.axis_size("seq")
+    owner = lax.axis_index("dp") * lax.axis_size("seq") + lax.axis_index("seq")
+    mod_rows = modulation_weight.shape[0]
     cond_float = conditioning.astype(jnp.float32)
     cond_act = jax.nn.silu(cond_float).astype(jnp.bfloat16)
-    gathered = (
-        lax.all_gather(qkv_weight, ("dp", "seq"), axis=0, tiled=True),
-        lax.all_gather(proj_weight, ("dp", "seq"), axis=0, tiled=True),
-        lax.all_gather(mlp_in_weight, ("dp", "seq"), axis=0, tiled=True),
-        lax.all_gather(mlp_out_weight, ("dp", "seq"), axis=0, tiled=True),
-        lax.all_gather(modulation_weight, ("dp", "seq"), axis=0, tiled=True),
-        lax.all_gather(qv_bias, ("dp", "seq"), axis=0, tiled=True),
-        lax.all_gather(proj_bias, ("dp", "seq"), axis=0, tiled=True),
-        lax.all_gather(mlp_in_bias, ("dp", "seq"), axis=0, tiled=True),
-        lax.all_gather(mlp_out_bias, ("dp", "seq"), axis=0, tiled=True),
-        lax.all_gather(modulation_bias, ("dp", "seq"), axis=0, tiled=True),
-    )
-    qkv_full, proj_full, in_full, out_full = (gathered[0], gathered[1], gathered[2], gathered[3])
-    qv_full, proj_bias_full, in_bias_full, out_bias_full = (
-        gathered[5],
-        gathered[6],
-        gathered[7],
-        gathered[8],
-    )
-    modulation = matmul(cond_act, gathered[4]) + gathered[9].astype(jnp.float32)
+    cond_all = lax.all_gather(cond_act, "dp", axis=0, tiled=True)
+    cond_own = lax.dynamic_slice_in_dim(cond_all, owner * mod_rows, mod_rows, axis=1)
+    mod_part = lax.psum_scatter(
+        matmul(cond_own, modulation_weight), "dp", scatter_dimension=0, tiled=True
+    )
+    biases = (qv_bias, proj_bias, mlp_in_bias, mlp_out_bias, modulation_bias)
+    joined = lax.all_gather(jnp.concatenate(biases), axes, axis=0)
+    bounds = [0]
+    for bias in biases:
+        bounds.append(bounds[-1] + bias.shape[0])
+    qv_full, proj_bias_full, in_bias_full, out_bias_full, mod_bias_full = [
+        joined[:, low:high].reshape(-1) for low, high in zip(bounds[:-1], bounds[1:])
+    ]
+    modulation = lax.psum(mod_part, "seq") + mod_bias_full.astype(jnp.float32)
+    qkv_full, proj_full, in_full, out_full = (
+        lax.all_gather(qkv_weight, axes, axis=0, tiled=True),
+        lax.all_gather(proj_weight, axes, axis=0, tiled=True),
+        lax.all_gather(mlp_in_weight, axes, axis=0, tiled=True),
+        lax.all_gather(mlp_out_weight, axes, axis=0, tiled=True),
+    )
     shift_attn, scale_attn, gate_attn, shift_mlp, scale_mlp, gate_mlp = [
         piece[:, None, :] for piece in jnp.split(modulation, 6, axis=1)
     ]
@@ -168,13 +180,7 @@
         lat_count, local_len, width
     )
     block_out = mid + gate_mlp * mlp_branch
-    back_qkv, back_proj, back_in, back_out, back_mod = (
-        lax.all_gather(qkv_weight, ("dp", "seq"), axis=0, tiled=True),
-        lax.all_gather(proj_weight, ("dp", "seq"), axis=0, tiled=True),
-        lax.all_gather(mlp_in_weight, ("dp", "seq"), axis=0, tiled=True),
-        lax.all_gather(mlp_out_weight, ("dp", "seq"), axis=0, tiled=True),
-        lax.all_gather(modulation_weight, ("dp", "seq"), axis=0, tiled=True),
-    )
+    back_qkv, back_proj, back_in, back_out = (qkv_full, proj_full, in_full, out_full)
     cot = out_cotangent.astype(jnp.float32)
     grad_gate_mlp = jnp.sum(cot * mlp_branch, axis=1)
     grad_mlp = (cot * gate_mlp).reshape(tokens, width)
@@ -254,40 +260,35 @@
     grad_modulation = lax.psum(grad_mod_part, "seq")
     sigma = jax.nn.sigmoid(cond_float)
     silu_slope = sigma * (1.0 + cond_float * (1.0 - sigma))
-    mod_blocks = jnp.split(grad_modulation, 6, axis=1)
-    weight_blocks = jnp.split(back_mod, 6, axis=1)
-    through = jnp.zeros((lat_count, width), jnp.float32)
-    for grad_block, weight_block in zip(mod_blocks, weight_blocks):
-        through = through + exact_right_t(grad_block, weight_block.astype(jnp.float32))
+    grad_mod_all = lax.all_gather(grad_modulation, "dp", axis=0, tiled=True)
+    through_own = exact_right_t(grad_mod_all, modulation_weight.astype(jnp.float32))
+    through_all = lax.all_gather(through_own, axes, axis=1, tiled=True)
+    through = lax.dynamic_slice_in_dim(
+        through_all, lax.axis_index("dp") * lat_count, lat_count, axis=0
+    )
     grad_conditioning = through * silu_slope
-    local_mod_weight = exact_left_t(cond_act.astype(jnp.float32), grad_mod_part)
-    local_mod_bias = jnp.sum(grad_mod_part, axis=0)
-    summed = (
-        lax.psum_scatter(grad_qkv_weight, ("dp", "seq"), scatter_dimension=0, tiled=True),
-        lax.psum_scatter(grad_proj_weight, ("dp", "seq"), scatter_dimension=0, tiled=True),
-        lax.psum_scatter(grad_in_weight, ("dp", "seq"), scatter_dimension=0, tiled=True),
-        lax.psum_scatter(grad_out_weight, ("dp", "seq"), scatter_dimension=0, tiled=True),
-        lax.psum_scatter(local_mod_weight, ("dp", "seq"), scatter_dimension=0, tiled=True),
-        lax.psum_scatter(grad_qv_bias, ("dp", "seq"), scatter_dimension=0, tiled=True),
-        lax.psum_scatter(grad_proj_bias, ("dp", "seq"), scatter_dimension=0, tiled=True),
-        lax.psum_scatter(grad_in_bias, ("dp", "seq"), scatter_dimension=0, tiled=True),
-        lax.psum_scatter(grad_out_bias, ("dp", "seq"), scatter_dimension=0, tiled=True),
-        lax.psum_scatter(local_mod_bias, ("dp", "seq"), scatter_dimension=0, tiled=True),
-    )
-    owned_qkv, owned_proj, owned_in, owned_out, grad_modulation_weight = (
-        summed[0],
-        summed[1],
-        summed[2],
-        summed[3],
-        summed[4],
-    )
-    owned_qv, owned_proj_bias, owned_in_bias, owned_out_bias, grad_modulation_bias = (
-        summed[5],
-        summed[6],
-        summed[7],
-        summed[8],
-        summed[9],
-    )
+    grad_modulation_weight = exact_left_t(cond_own.astype(jnp.float32), grad_mod_all)
+    bias_rows = modulation_bias.shape[0]
+    grad_modulation_bias = lax.dynamic_slice_in_dim(
+        jnp.sum(grad_mod_all, axis=0), owner * bias_rows, bias_rows, axis=0
+    )
+    owned_out, owned_in, owned_proj, owned_qkv = (
+        reduce_rows(grad_out_weight),
+        reduce_rows(grad_in_weight),
+        reduce_rows(grad_proj_weight),
+        reduce_rows(grad_qkv_weight),
+    )
+    bias_grads = jnp.concatenate(
+        [
+            grad.reshape(parts, -1)
+            for grad in (grad_qv_bias, grad_proj_bias, grad_in_bias, grad_out_bias)
+        ],
+        axis=1,
+    )
+    owned_biases = lax.psum_scatter(bias_grads, axes, scatter_dimension=0, tiled=True)[0]
+    owned_qv, owned_proj_bias, owned_in_bias, owned_out_bias = [
+        owned_biases[low:high] for low, high in zip(bounds[:4], bounds[1:5])
+    ]
     return (
         block_out,
         grad_latents,

time: 1130 us -> 684 us (0.61)
  waiting for transfers between devices: 836 us -> 312 us
  blocking collectives: 140 us -> 241 us
  matrix products: 95.5 us -> 69.2 us
    reduce_scatter x5 -> x8, waiting for transfers between devices: 570 us -> 123 us  [the longest x4 102 us: reduce_rows(): lax.psum_scatter(grad.astype(jnp.bfloat16), 'dp', scatter_dimension=0, ti...]
    all_gather x5 -> x4, waiting for transfers between devices: 215 us -> 119 us  [the longest x1 61.4 us: local(): lax.all_gather(mlp_out_weight, axes, axis=0, tiled=True)]
    all_gather x0 -> x3, blocking collectives: none -> 89.8 us  [the longest x1 69.1 us: local(): through_all = lax.all_gather(through_own, axes, axis=1, tiled=True)]
    psum x0 -> x1, blocking collectives: none -> 19.3 us  [local(): modulation = lax.psum(mod_part, 'seq') + mod_bias_full.astype(jnp.float32)]
    dot_general x6 -> x1, matrix products: 14.6 us -> 0.32 us  [exact_right_t(): lax.dot_general(left, right, (((1,), (1,)), ((), ())), precision=lax.Prec...]
  transfers between devices with their start and end apart: 12 -> 15, of which waited for: 11 -> 8; matrix products, arithmetic and copies ran while one was open for 8% -> 13% of each run, Pallas kernels for 0% -> 0%
where the time goes in v1:
time: 684 us; the launch traced here: 683 us
  waiting for transfers between devices  312 us (46%)
  blocking collectives  241 us (35%)
  matrix products  69.2 us (10%)
  local copies, waits for them, and re-layouts  26.8 us (4%)
  between operations  16.9 us (2%)
  other arithmetic  16.5 us (2%)
    reduce_scatter x4, waiting for transfers between devices, reduce_rows(): lax.psum_scatter(grad.astype(jnp.bfloat16), 'dp', scatter_dimension=0, ti...  102 us
    unnamed x2, blocking collectives  77.4 us
    all_gather x1, blocking collectives, local(): through_all = lax.all_gather(through_own, axes, axis=1, tiled=True)  69.1 us
    all_gather x1, waiting for transfers between devices, local(): lax.all_gather(mlp_out_weight, axes, axis=0, tiled=True)  61.4 us
    all_gather x1, waiting for transfers between devices, local(): lax.all_gather(mlp_in_weight, axes, axis=0, tiled=True)  57.8 us
    reduce_scatter x1, waiting for transfers between devices, local(): lax.psum_scatter(grad_values_all.reshape(lat_count, -1, width), 'seq', sc...  35.3 us
    reduce_scatter x4, waiting for transfers between devices, reduce_rows(): across = lax.psum_scatter(within, 'seq', scatter_dimension=0, tiled=True)  21.3 us
    reduce_scatter x1, waiting for transfers between devices, local(): lax.psum_scatter(grad_keys_all.reshape(lat_count, -1, width), 'seq', scat...  21 us
  transfers between devices with their start and end apart: 15, of which 8 were waited for; matrix products, arithmetic and copies ran while one was open for 13% of the time, Pallas kernels for 0%

profile of v1, /device:TPU:0, one launch (start us, length us, event | category | flops | bytes accessed | tf_op | source)
XLA Modules:
  0.0 683.4 jit_solution(10275414804276504598)
XLA Ops:
  8.9 10.6 %all-gather.1 = bf16[8,2,768]{2,1,0:T(2,128)(2,1)S(1)} all-gather(bf16[1,2,768]{2,1,0:T(2,128)(2,1)S(1)} %fusion.66), channel_id=1, replica_groups=mesh['dp'=8,'seq'=4] {'dp'}, dimensions={0}, use_global_device_ids=true | all-gather | bytes 27648 | tf_op jit(solution)/shard_map/all_gather | solution.py:107
  23.1 3.4 concatenate.21
  26.8 40.1 %all-reduce = bf16[10752]{0:T(1024)(128)(2,1)S(1)} all-reduce(bf16[10752]{0:T(1024)(128)(2,1)S(1)} %dynamic-update-slice), channel_id=2, replica_groups=mesh['dp'=8,'seq'=4] {'dp','seq'}, use_global_device_ids=true, to_apply=%add | all-reduce | flops 10752 | bytes 43008
  69.3 10.3 %all-reduce.5.cloned.1.call-done = f32[16,4608]{1,0:T(8,128)} async-done(((f32[16,4608]{1,0:T(8,128)}), f32[16,4608]{1,0:T(8,128)}) %all-reduce.5.cloned.1.call-update) | async-done | bytes 294928
  80.5 19.3 %psum.14 = f32[2,4608]{1,0:T(2,128)S(1)} all-reduce(f32[2,4608]{1,0:T(2,128)S(1)} %constant_dynamic-slice_fusion), channel_id=1, replica_groups=mesh['dp'=8,'seq'=4] {'seq'}, use_global_device_ids=true, to_apply=%region_1.2 | all-reduce | flops 9216 | bytes 73728 | tf_op jit(solution)/shard_map/psum | solution.py:120
  100.1 2.7 fusion.84
  103.6 18.0 %all_gather.38 = bf16[2,256,768]{2,1,0:T(8,128)(2,1)S(1)} all-gather(bf16[2,64,768]{2,1,0:T(8,128)(2,1)S(1)} %bitcast.118), channel_id=1, replica_groups=mesh['dp'=8,'seq'=4] {'seq'}, dimensions={1}, use_global_device_ids=true | all-gather | bytes 983040 | tf_op jit(solution)/shard_map/all_gather | solution.py:151
  121.6 1.2 copy.50
  122.8 17.3 %all_gather.37 = bf16[2,256,768]{2,1,0:T(8,128)(2,1)S(1)} all-gather(bf16[2,64,768]{2,1,0:T(8,128)(2,1)S(1)} %bitcast.117), channel_id=1, replica_groups=mesh['dp'=8,'seq'=4] {'seq'}, dimensions={1}, use_global_device_ids=true | all-gather | bytes 983040 | tf_op jit(solution)/shard_map/all_gather | solution.py:152
  140.4 1.9 fusion.80
  144.1 1.7 convolution_add_fusion.1
  147.6 57.8 %all-gather.13.cloned.1.call-done = bf16[768,3072]{1,0:T(8,128)(2,1)} async-done(((bf16[24,3072]{1,0:T(8,128)(2,1)}), bf16[768,3072]{1,0:T(8,128)(2,1)}) %all-gather.13.cloned.1.call-update) | async-done | bytes 4718608 | tf_op jit(solution)/shard_map/all_gather | solution.py:124
  205.4 3.2 convolution_add_fusion
  208.7 61.4 %all-gather.15.cloned.1.call-done = bf16[3072,768]{1,0:T(8,128)(2,1)} async-done(((bf16[96,768]{1,0:T(8,128)(2,1)}), bf16[3072,768]{1,0:T(8,128)(2,1)}) %all-gather.15.cloned.1.call-update) | async-done | bytes 4718608 | tf_op jit(solution)/shard_map/all_gather | solution.py:125
  270.0 4.5 fusion.83
  274.5 2.5 fusion.46
  277.1 1.5 fusion.47
  278.6 3.5 convolution_add_fusion.2
  284.7 1.5 convolution_convert_fusion.3
  286.5 2.6 convolution_convert_fusion.5
  289.1 2.1 reshape.252
  291.1 2.1 copy.58
  293.3 2.9 fusion.85
  296.2 11.6 %fusion.10 = f32[2,12,64,256]{3,2,1,0:T(8,128)} fusion(bf16[2,64,12,64]{1,3,2,0:T(8,128)(2,1)} %copy-done.21, f32[2,12,64,256]{3,2,1,0:T(8,128)} %fusion.85, f32[2,12,64,256]{3,2,1,0:T(8,128)S(1)} %get-tuple-element.48, f32[2,12,64]{2,1,0:T(8,128)S(1)} %log_add_fusion), kind=kOutput, calls=%fused_computation.20 | convolution fusion | flops 53085952 | bytes 4921344 | tf_op jit(solution)/shard_map/bhqk,bqhd->bkhd/dot_general | solution.py:225
  307.8 3.0 copy.57
  310.9 2.6 fusion.52
  313.5 3.0 copy.59
  316.6 4.7 convolution_convert_fusion
  322.5 3.5 convolution_convert_fusion.1
  326.1 1.1 copy-done.14
  327.2 10.4 %fusion.76 = (f32[12,64]{1,0:T(8,128)S(1)}, bf16[2,64,12,64]{3,1,2,0:T(8,128)(2,1)S(1)}) fusion(bf16[2,256,12,64]{1,3,2,0:T(8,128)(2,1)S(1)} %bitcast.107, f32[2,12,64,256]{3,2,1,0:T(8,128)} %fusion.85, f32[2,12,64,256]{3,2,1,0:T(8,128)S(1)} %get-tuple-element.48, f32[2,12,64]{2,1,0:T(8,128)S(1)} %log_add_fusion), kind=kOutput, calls=%fused_computation.138 | convolution fusion | flops 53281792 | bytes 4137984 | tf_op jit(solution)/shard_map/bhqk,bkhd->bqhd/dot_general | solution.py:218
  338.2 21.0 %reduce-scatter.11.cloned.1.call-done = f32[2,64,768]{2,1,0:T(8,128)} async-done(((f32[2,256,768]{2,1,0:T(8,128)}), f32[2,64,768]{2,1,0:T(8,128)}) %reduce-scatter.11.cloned.1.call-update) | async-done | bytes 393232 | tf_op jit(solution)/shard_map/reduce_scatter | solution.py:229
  360.3 35.3 %reduce-scatter.13.cloned.1.call-done = f32[2,64,768]{2,1,0:T(8,128)} async-done(((f32[2,256,768]{2,1,0:T(8,128)}), f32[2,64,768]{2,1,0:T(8,128)}) %reduce-scatter.13.cloned.1.call-update) | async-done | bytes 393232 | tf_op jit(solution)/shard_map/reduce_scatter | solution.py:232
  395.6 1.2 fusion.77
  397.0 2.9 convolution_convert_fusion.2
  400.2 51.4 %reduce-scatter.27.cloned.1.call-done = bf16[384,768]{1,0:T(8,128)(2,1)} async-done(((bf16[3072,768]{1,0:T(8,128)(2,1)}), bf16[384,768]{1,0:T(8,128)(2,1)}) %reduce-scatter.27.cloned.1.call-update) | async-done | bytes 589840 | tf_op jit(solution)/shard_map/reduce_scatter | solution.py:75
  452.0 21.3 %reduce-scatter.21.cloned.1.call-done = bf16[24,768]{1,0:T(8,128)(2,1)} async-done(((bf16[96,768]{1,0:T(8,128)(2,1)}), bf16[24,768]{1,0:T(8,128)(2,1)}) %reduce-scatter.21.cloned.1.call-update) | async-done | bytes 36880 | tf_op jit(solution)/shard_map/reduce_scatter | solution.py:78
  473.3 1.4 convert_element_type.162
  474.7 3.4 fusion.45
  478.4 50.3 %reduce-scatter.23.cloned.1.call-done = bf16[96,3072]{1,0:T(8,128)(2,1)} async-done(((bf16[768,3072]{1,0:T(8,128)(2,1)}), bf16[96,3072]{1,0:T(8,128)(2,1)}) %reduce-scatter.23.cloned.1.call-update) | async-done | bytes 589840 | tf_op jit(solution)/shard_map/reduce_scatter | solution.py:75
  528.9 19.5 %psum.15 = f32[2,4608]{1,0:T(2,128)S(1)} all-reduce(f32[2,4608]{1,0:T(2,128)S(1)} %constant_dynamic-update-slice_fusion), channel_id=1, replica_groups=mesh['dp'=8,'seq'=4] {'seq'}, use_global_device_ids=true, to_apply=%region_21.22 | all-reduce | flops 9216 | bytes 73728 | tf_op jit(solution)/shard_map/psum | solution.py:260
  548.4 10.1 %all-gather.2 = f32[8,2,4608]{2,1,0:T(2,128)S(1)} all-gather(f32[1,2,4608]{2,1,0:T(2,128)S(1)} %bitcast.121), channel_id=1, replica_groups=mesh['dp'=8,'seq'=4] {'dp'}, dimensions={0}, use_global_device_ids=true | all-gather | bytes 331776 | tf_op jit(solution)/shard_map/all_gather | solution.py:263
  558.8 37.3 %all-reduce.2 = f32[32,192]{1,0:T(8,128)S(1)} all-reduce(f32[32,192]{1,0:T(8,128)S(1)} %pad_maximum_fusion.3), channel_id=8, replica_groups=mesh['dp'=8,'seq'=4] {'dp','seq'}, use_global_device_ids=true, to_apply=%region_30.31.clone | all-reduce | flops 6144 | bytes 49152
  597.8 69.1 %all-gather.3 = f32[32,24,16]{1,2,0:T(8,128)S(1)} all-gather(f32[1,24,16]{1,2,0:T(8,128)S(1)} %convolution_bitcast_fusion), channel_id=1, replica_groups=mesh['dp'=8,'seq'=4] {'dp','seq'}, dimensions={0}, use_global_device_ids=true | all-gather | bytes 50688 | tf_op jit(solution)/shard_map/all_gather | solution.py:265
  669.0 1.2 fusion.62
  671.1 1.6 convert_element_type.166
  672.8 1.6 convert_element_type.164
  674.4 1.6 convert_element_type.160
  (166 shorter events, 24.2 us)
Async XLA Ops:
  8.0 11.5 %copy-start = (bf16[24,4608]{1,0:T(8,128)(2,1)S(1)}, bf16[24,4608]{1,0:T(8,128)(2,1)}, u32[]{:S(2)}) copy-start(bf16[24,4608]{1,0:T(8,128)(2,1)} %param.16) | copy-start | bytes 663556
  8.0 59.7 %copy-start.25 = (u32[32]{0:T(128)S(1)}, u32[32]{0:T(128)}, u32[]{:S(2)}) copy-start(u32[32]{0:T(128)} %constant.74) | copy-start | bytes 388
  8.0 60.9 %copy-start.5 = (bf16[2,64,768]{2,1,0:T(8,128)(2,1)S(1)}, bf16[2,64,768]{2,1,0:T(8,128)(2,1)}, u32[]{:S(2)}) copy-start(bf16[2,64,768]{2,1,0:T(8,128)(2,1)} %param.13) | copy-start | bytes 589828
  8.1 71.5 %all-reduce.5.cloned.1.call-start = ((), (), s32[]{:S(2)}) async-start(), calls=%async_computation.24 | async-start | bytes 589824
  20.5 79.5 %all-gather.9.cloned.1.call-start = ((), (), s32[]{:S(2)}) async-start(), calls=%async_computation.10 | async-start | bytes 3649536 | tf_op jit(solution)/shard_map/all_gather | solution.py:122
  21.1 122.9 %all-gather.11.cloned.1.call-start = ((), (), s32[]{:S(2)}) async-start(), calls=%async_computation.11 | async-start | bytes 1216512 | tf_op jit(solution)/shard_map/all_gather | solution.py:123
  21.7 183.7 %all-gather.13.cloned.1.call-start = ((), (), s32[]{:S(2)}) async-start(), calls=%async_computation.12 | async-start | bytes 4866048 | tf_op jit(solution)/shard_map/all_gather | solution.py:124
  22.3 247.8 %all-gather.15.cloned.1.call-start = ((), (), s32[]{:S(2)}) async-start(), calls=%async_computation.13 | async-start | bytes 4866048 | tf_op jit(solution)/shard_map/all_gather | solution.py:125
  23.0 298.4 %reduce-scatter.19.cloned.1.call-start = ((), (), s32[]{:S(2)}) async-start(), calls=%async_computation.18 | async-start | bytes 1327104 | tf_op jit(solution)/shard_map/reduce_scatter | solution.py:75
  100.0 2.8 copy-start.16
  103.6 36.8 %copy-start.21 = (bf16[2,64,12,64]{1,3,2,0:T(8,128)(2,1)}, bf16[2,64,12,64]{1,3,2,0:T(8,128)(2,1)S(1)}, u32[]{:S(2)}) copy-start(bf16[2,64,12,64]{1,3,2,0:T(8,128)(2,1)S(1)} %copy.56) | copy-start | bytes 589828
  140.4 2.5 copy-start.4
  144.0 2.2 copy-start.18
  144.0 2.7 copy-start.22
  145.8 59.6 %copy-start.8 = (f32[128,768]{1,0:T(8,128)}, f32[128,768]{1,0:T(8,128)S(1)}, u32[]{:S(2)}) copy-start(f32[128,768]{1,0:T(8,128)S(1)} %convolution_add_fusion.1) | copy-start | bytes 1179652
  146.0 0.8 copy-start.2
  270.0 4.5 copy-start.1
  274.5 2.5 copy-start.12
  278.6 3.6 copy-start.3
  278.6 3.6 copy-start.7
  278.6 3.6 copy-start.9
  278.6 3.6 copy-start.23
  282.2 2.5 copy-start.19
  283.2 0.7 copy-start.10
  284.0 0.7 copy-start.20
  286.2 73.0 %reduce-scatter.11.cloned.1.call-start = ((), (), s32[]{:S(2)}) async-start(), calls=%async_computation.14 | async-start | bytes 1966080 | tf_op jit(solution)/shard_map/reduce_scatter | solution.py:229
  310.8 84.8 %reduce-scatter.13.cloned.1.call-start = ((), (), s32[]{:S(2)}) async-start(), calls=%async_computation.15 | async-start | bytes 1966080 | tf_op jit(solution)/shard_map/reduce_scatter | solution.py:232
  316.5 135.1 %reduce-scatter.27.cloned.1.call-start = ((), (), s32[]{:S(2)}) async-start(), calls=%async_computation.22 | async-start | bytes 5308416 | tf_op jit(solution)/shard_map/reduce_scatter | solution.py:75
  321.3 1.1 copy-start.13
  321.3 1.2 copy-start.15
  321.4 151.9 %reduce-scatter.21.cloned.1.call-start = ((), (), s32[]{:S(2)}) async-start(), calls=%async_computation.19 | async-start | bytes 184320 | tf_op jit(solution)/shard_map/reduce_scatter | solution.py:78
  321.9 206.8 %reduce-scatter.23.cloned.1.call-start = ((), (), s32[]{:S(2)}) async-start(), calls=%async_computation.20 | async-start | bytes 5308416 | tf_op jit(solution)/shard_map/reduce_scatter | solution.py:75
  326.0 1.1 copy-start.14
  326.1 270.9 %reduce-scatter.15.cloned.1.call-start = ((), (), s32[]{:S(2)}) async-start(), calls=%async_computation.16 | async-start | bytes 3981312 | tf_op jit(solution)/shard_map/reduce_scatter | solution.py:75
  337.6 59.4 %copy-start.17 = (bf16[2,64,768]{2,1,0:T(8,128)(2,1)S(1)}, bf16[2,64,768]{2,1,0:T(8,128)(2,1)}, u32[]{:S(2)}) copy-start(bf16[2,64,768]{2,1,0:T(8,128)(2,1)} %copy-done.16) | copy-start | bytes 589828
  399.9 271.2 %reduce-scatter.29.cloned.1.call-start = ((), (), s32[]{:S(2)}) async-start(), calls=%async_computation.23 | async-start | bytes 737280 | tf_op jit(solution)/shard_map/reduce_scatter | solution.py:78
  451.7 221.1 %reduce-scatter.25.cloned.1.call-start = ((), (), s32[]{:S(2)}) async-start(), calls=%async_computation.21 | async-start | bytes 737280 | tf_op jit(solution)/shard_map/reduce_scatter | solution.py:78
  474.7 3.4 copy-start.6
  528.8 145.7 %reduce-scatter.17.cloned.1.call-start = ((), (), s32[]{:S(2)}) async-start(), calls=%async_computation.17 | async-start | bytes 552960 | tf_op jit(solution)/shard_map/reduce_scatter | solution.py:78
  558.5 109.9 %copy-start.24 = (bf16[2,768]{1,0:T(2,128)(2,1)S(1)}, bf16[2,768]{1,0:T(2,128)(2,1)}, u32[]{:S(2)}) copy-start(bf16[2,768]{1,0:T(2,128)(2,1)} %param.14) | copy-start | bytes 9220
  596.6 73.6 %copy-start.11 = (f32[2,64,768]{2,1,0:T(8,128)S(1)}, f32[2,64,768]{2,1,0:T(8,128)}, u32[]{:S(2)}) copy-start(f32[2,64,768]{2,1,0:T(8,128)} %copy-done.10) | copy-start | bytes 1179652
Sparse Core Ops, SparseCore 0:
  20.6 58.8 all-reduce.4
  286.3 35.0 reduce-scatter.18
  323.7 35.4 reduce-scatter.10
  361.3 34.2 reduce-scatter.12
  398.9 52.6 reduce-scatter.26
  453.7 19.5 reduce-scatter.20
  476.7 51.9 reduce-scatter.22
  532.2 48.4 reduce-scatter.14
  583.0 22.1 reduce-scatter.28
  607.3 21.2 reduce-scatter.24
  631.0 19.7 reduce-scatter.16
Sparse Core Ops, SparseCore 1:
  23.8 60.4 all-gather.8
  86.9 53.4 all-gather.10
  143.1 62.3 all-gather.12
  208.2 61.7 all-gather.14
